TPU v7x, 32 devices: a whole 2x2x4 slice. The times are simulated.
32 devices in a mesh: row: 4 (over y, x), col: 8 (over z, core).
Axes of the slice: x: 2, y: 2, z: 4, core: 2. Of those that a mesh axis runs over, the one named last changes fastest.
Arguments:
- noise: float32 [2048, 3072], P('row', 'col'), may hold values from -30 to 30
- images: float32 [6144, 3072], P('col', 'row'), may hold values from -6 to 6
- time_index: int32 [2048], P('row'), may hold values from 0 to 999
- w_in: float32 [3072, 3072], P(None, 'col'), may hold values from -0.109375 to 0.109375
- time_gain: float32 [3072], P('col'), may hold values from -5 to 5
- w_out: float32 [3072, 3072], P('col'), may hold values from -0.109375 to 0.109375
Outputs:
- targets: float32 [2048, 3072], P('row', 'col')
- row_pot: float32 [2048], P('row')
- col_pot: float32 [6144], P('col')
- grad_in: float32 [3072, 3072], P('row', 'col')
- grad_time: float32 [3072], P('col')
- grad_out: float32 [3072, 3072], P('col', 'row')
- mse: float32 [], replicated
All inputs are finite; a program needn't handle non-finite values.
Results may differ from a plain program's by a relative error of at most 0.0003.
Values sent between devices are 32-bit elements; how exact they have to be, the bound alone decides.
A program may use at most 128 MiB of HBM per device.

v0:
```python
import jax
import jax.numpy as jnp
from jax import lax
from jax.sharding import PartitionSpec as P

ITERS = 2
TIMES = 1000
EPSILON = 0.01


def merged(array, axis, combine):
    everything = jax.tree.map(lambda part: lax.all_gather(part, axis), array)
    first = jax.tree.map(lambda part: part[0], everything)

    def hop(k, so_far):
        return combine(so_far, jax.tree.map(lambda part: part[k], everything))

    return lax.fori_loop(1, lax.axis_size(axis), hop, first)


def joined(left_pair, right_pair):
    peak = jnp.maximum(left_pair[0], right_pair[0])
    total = left_pair[1] * jnp.exp(left_pair[0] - peak) + right_pair[1] * jnp.exp(
        right_pair[0] - peak
    )
    return (peak, total)


def over_images(logits):
    local_peak = jnp.max(logits, axis=1)
    local_total = jnp.sum(jnp.exp(logits - local_peak[:, None]), axis=1)
    peak, total = merged((local_peak, local_total), "col", joined)
    return (peak, total)


def over_noise(logits):
    local_peak = jnp.max(logits, axis=0)
    local_total = jnp.sum(jnp.exp(logits - local_peak[None, :]), axis=0)
    peak, total = merged((local_peak, local_total), "row", joined)
    return (peak, total)


def body(noise, images, time_index, w_in, time_gain, w_out):
    highest = lax.Precision.HIGHEST
    full_noise = lax.all_gather(noise, "col", axis=1, tiled=True)
    full_images = lax.all_gather(images, "row", axis=1, tiled=True)
    width = full_noise.shape[1]
    noise_count = full_noise.shape[0] * lax.axis_size("row")
    image_count = full_images.shape[0] * lax.axis_size("col")
    noise_norms = jnp.sum(full_noise * full_noise, axis=1)
    image_norms = jnp.sum(full_images * full_images, axis=1)
    cross = lax.dot_general(
        full_noise,
        full_images,
        (((1,), (1,)), ((), ())),
        precision=highest,
        preferred_element_type=jnp.float32,
    )
    scaled = (noise_norms[:, None] + image_norms[None, :] - 2.0 * cross) / (width * EPSILON)
    col_pot = jnp.zeros((full_images.shape[0],), jnp.float32)
    row_pot = jnp.zeros((full_noise.shape[0],), jnp.float32)
    for iteration in range(ITERS):
        peak, total = over_images(col_pot[None, :] - scaled)
        row_pot = jnp.log(jnp.float32(image_count)) - (jnp.log(total) + peak)
        peak, total = over_noise(row_pot[:, None] - scaled)
        col_pot = jnp.log(jnp.float32(noise_count)) - (jnp.log(total) + peak)
    logits = col_pot[None, :] - scaled
    peak, total = over_images(logits)
    weights = jnp.exp(logits - (jnp.log(total) + peak)[:, None])
    partial_value = jnp.dot(
        weights, full_images, precision=highest, preferred_element_type=jnp.float32
    )
    slice_width = noise.shape[1]
    slice_start = lax.axis_index("col") * slice_width
    whole_targets = lax.psum(partial_value, "col")
    targets = lax.dynamic_slice_in_dim(whole_targets, slice_start, slice_width, 1)
    fraction = (time_index.astype(jnp.float32) + 0.5) / TIMES
    mixed = (1.0 - fraction)[:, None] * full_noise + fraction[:, None] * whole_targets
    velocity = whole_targets - full_noise
    pre = (
        jnp.dot(mixed, w_in, precision=highest, preferred_element_type=jnp.float32)
        + fraction[:, None] * time_gain[None, :]
    )
    sigma = jax.nn.sigmoid(pre)
    hidden = pre * sigma
    part_out = jnp.dot(hidden, w_out, precision=highest, preferred_element_type=jnp.float32)
    out = lax.psum(part_out, "col")
    diff = out - velocity
    squared = jnp.sum(diff * diff)
    slope = diff / jnp.sqrt(jnp.float32(noise_count))
    local_out = lax.dot_general(
        hidden,
        slope,
        (((0,), (0,)), ((), ())),
        precision=highest,
        preferred_element_type=jnp.float32,
    )
    back = lax.dot_general(
        slope,
        w_out,
        (((1,), (1,)), ((), ())),
        precision=highest,
        preferred_element_type=jnp.float32,
    )
    dpre = back * sigma * (1.0 + pre * (1.0 - sigma))
    local_in = lax.dot_general(
        mixed, dpre, (((0,), (0,)), ((), ())), precision=highest, preferred_element_type=jnp.float32
    )
    local_time = jnp.sum(fraction[:, None] * dpre, axis=0)
    grad_in, grad_out = (
        lax.psum_scatter(local_in, "row", scatter_dimension=0, tiled=True),
        lax.psum_scatter(local_out, "row", scatter_dimension=1, tiled=True),
    )
    grad_time, squared_all = lax.psum((local_time, squared), "row")
    mse = squared_all / (noise_count * width)
    return (targets, row_pot, col_pot, grad_in, grad_time, grad_out, mse)


def solution(mesh):
    placed = (P("row", "col"), P("col", "row"), P("row"), P(None, "col"), P("col"), P("col", None))
    return jax.shard_map(
        body,
        mesh=mesh,
        in_specs=placed,
        out_specs=(
            P("row", "col"),
            P("row"),
            P("col"),
            P("row", "col"),
            P("col"),
            P("col", "row"),
            P(),
        ),
        check_vma=False,
    )
```

profile of v0, /device:TPU:0, one launch (start us, length us, event | category | flops | bytes accessed | tf_op | source)
XLA Modules:
  0.0 786.1 jit_solution(18099109052659360453)
XLA Ops:
  7.2 0.7 all-gather.23.cloned.1.call-update
  7.9 0.7 all-gather.25.cloned.1.call-update
  8.7 68.3 %all-gather.23.cloned.1.call-done = f32[512,3072]{1,0:T(8,128)} async-done(((f32[512,384]{1,0:T(8,128)}), f32[512,3072]{1,0:T(8,128)}) %all-gather.23.cloned.1.call-update) | async-done | bytes 6291472 | tf_op jit(solution)/shard_map/all_gather | solution.py:45
  77.0 3.3 multiply_reduce_fusion.2
  80.3 93.5 %all-gather.25.cloned.1.call-done = f32[768,3072]{1,0:T(8,128)} async-done(((f32[768,768]{1,0:T(8,128)}), f32[768,3072]{1,0:T(8,128)}) %all-gather.25.cloned.1.call-update) | async-done | bytes 9437200 | tf_op jit(solution)/shard_map/all_gather | solution.py:46
  173.8 4.5 multiply_reduce_fusion
  178.3 1.0 copy-done
  179.2 18.3 %subtract_reduce_fusion.3 = (f32[512]{0:T(512)S(1)}, f32[512,768]{1,0:T(8,128)S(1)}) fusion(f32[512,3072]{1,0:T(8,128)S(1)} %copy-done, f32[768,3072]{1,0:T(8,128)} %all-gather.25.cloned.1.call-done, f32[768]{0:T(1024)S(1)} %multiply_reduce_fusion, f32[512]{0:T(512)S(1)} %multiply_reduce_fusion.2), kind=kOutput, calls=%fused_computation.38 | convolution fusion | flops 14497873920 | bytes 17308672 | tf_op jit(solution)/shard_map/dot_general | solution.py:52
  197.5 0.4 exponential_reduce_fusion.4
  197.9 12.8 %all-gather.11 = f32[8,1,512]{2,1,0:T(1,128)S(1)} all-gather(f32[1,1,512]{2,1,0:T(1,128)S(1)} %bitcast.95), channel_id=3, replica_groups=mesh['row'=4,'col'=8] {'col'}, dimensions={0}, use_global_device_ids=true | all-gather | bytes 18432 | tf_op jit(solution)/shard_map/all_gather | solution.py:12
  210.8 12.8 %all-gather.10 = f32[8,1,512]{2,1,0:T(1,128)S(1)} all-gather(f32[1,1,512]{2,1,0:T(1,128)S(1)} %bitcast.93), channel_id=2, replica_groups=mesh['row'=4,'col'=8] {'col'}, dimensions={0}, use_global_device_ids=true | all-gather | bytes 18432 | tf_op jit(solution)/shard_map/all_gather | solution.py:12
  223.5 0.4 while.85
  224.1 0.3 exponential_reduce_fusion.3
  224.5 8.1 %all-gather.13 = f32[4,1,768]{2,1,0:T(1,128)S(1)} all-gather(f32[1,1,768]{2,1,0:T(1,128)S(1)} %reshape.65), channel_id=5, replica_groups=mesh['row'=4,'col'=8] {'row'}, dimensions={0}, use_global_device_ids=true | all-gather | bytes 15360 | tf_op jit(solution)/shard_map/all_gather | solution.py:12
  232.6 7.2 all-gather.12
  239.9 0.2 while.86
  240.3 0.4 exponential_reduce_fusion.2
  240.7 12.8 %all-gather.15 = f32[8,1,512]{2,1,0:T(1,128)S(1)} all-gather(f32[1,1,512]{2,1,0:T(1,128)S(1)} %bitcast.94), channel_id=7, replica_groups=mesh['row'=4,'col'=8] {'col'}, dimensions={0}, use_global_device_ids=true | all-gather | bytes 18432 | tf_op jit(solution)/shard_map/all_gather | solution.py:12
  253.5 12.8 %all-gather.14 = f32[8,1,512]{2,1,0:T(1,128)S(1)} all-gather(f32[1,1,512]{2,1,0:T(1,128)S(1)} %bitcast.91), channel_id=6, replica_groups=mesh['row'=4,'col'=8] {'col'}, dimensions={0}, use_global_device_ids=true | all-gather | bytes 18432 | tf_op jit(solution)/shard_map/all_gather | solution.py:12
  266.3 0.4 while.87
  266.9 0.3 exponential_reduce_fusion.1
  267.2 8.1 %all-gather.17 = f32[4,1,768]{2,1,0:T(1,128)S(1)} all-gather(f32[1,1,768]{2,1,0:T(1,128)S(1)} %reshape.73), channel_id=9, replica_groups=mesh['row'=4,'col'=8] {'row'}, dimensions={0}, use_global_device_ids=true | all-gather | bytes 15360 | tf_op jit(solution)/shard_map/all_gather | solution.py:12
  275.4 18.3 %all-gather.16 = f32[4,1,768]{2,1,0:T(1,128)S(1)} all-gather(f32[1,1,768]{2,1,0:T(1,128)S(1)} %reshape.71), channel_id=8, replica_groups=mesh['row'=4,'col'=8] {'row'}, dimensions={0}, use_global_device_ids=true | all-gather | bytes 15360 | tf_op jit(solution)/shard_map/all_gather | solution.py:12
  293.7 0.2 while.88
  293.9 0.2 subtract_reduce_fusion.4
  294.1 0.4 exponential_reduce_fusion
  294.6 12.8 %all-gather.19 = f32[8,1,512]{2,1,0:T(1,128)S(1)} all-gather(f32[1,1,512]{2,1,0:T(1,128)S(1)} %bitcast.96), channel_id=11, replica_groups=mesh['row'=4,'col'=8] {'col'}, dimensions={0}, use_global_device_ids=true | all-gather | bytes 18432 | tf_op jit(solution)/shard_map/all_gather | solution.py:12
  307.3 12.8 %all-gather.18 = f32[8,1,512]{2,1,0:T(1,128)S(1)} all-gather(f32[1,1,512]{2,1,0:T(1,128)S(1)} %bitcast.92), channel_id=10, replica_groups=mesh['row'=4,'col'=8] {'col'}, dimensions={0}, use_global_device_ids=true | all-gather | bytes 18432 | tf_op jit(solution)/shard_map/all_gather | solution.py:12
  320.1 0.4 while.89
  320.5 19.3 %fusion.6 = f32[512,3072]{1,0:T(8,128)} fusion(f32[768,3072]{1,0:T(8,128)} %all-gather.25.cloned.1.call-done, f32[512,768]{1,0:T(8,128)S(1)} %get-tuple-element.759, f32[512]{0:T(512)S(1)} %log_add_fusion, f32[768]{0:T(1024)S(1)} %add_subtract_fusion), kind=kOutput, calls=%fused_computation.26 | convolution fusion | flops 14496301056 | bytes 17306624 | tf_op jit(solution)/shard_map/dot_general | solution.py:70
  339.9 0.6 copy-done.6
  340.4 133.1 %all-reduce.4.cloned.1.call-done = f32[512,3072]{1,0:T(8,128)} async-done(((f32[512,3072]{1,0:T(8,128)}), f32[512,3072]{1,0:T(8,128)}) %all-reduce.4.cloned.1.call-update) | async-done | bytes 6291472 | tf_op jit(solution)/shard_map/psum | solution.py:75
  473.6 14.6 %convolution_add_fusion = f32[512,384]{1,0:T(8,128)S(1)} fusion(f32[3072,384]{1,0:T(8,128)} %param.19, f32[384]{0:T(512)S(1)} %copy-done.7, f32[512]{0:T(512)S(1)} %get-tuple-element.757, f32[512,3072]{1,0:T(8,128)} %all-reduce.4.cloned.1.call-done, f32[512,3072]{1,0:T(8,128)} %all-gather.23.cloned.1.call-done, f32[512]{0:T(512)S(1)} %get-tuple-element.756), kind=kOutput, calls=%fused_computation.43 | convolution fusion | flops 7252869120 | bytes 18093568 | tf_op jit(solution)/shard_map/dot_general | solution.py:81
  488.2 0.9 copy-done.2
  489.1 12.0 %fusion.20 = f32[512,3072]{1,0:T(8,128)} fusion(f32[384,3072]{1,0:T(8,128)S(1)} %bitcast.68, f32[512,384]{1,0:T(8,128)S(1)} %convolution_add_fusion), kind=kOutput, calls=%fused_computation.49 | convolution fusion | flops 7248543744 | bytes 11796480 | tf_op jit(solution)/shard_map/dot_general | solution.py:86
  501.1 0.3 reduce-scatter.5.cloned.1.call-start
  501.4 136.0 %all-reduce.6.cloned.1.call-done = f32[512,3072]{1,0:T(8,128)} async-done(((f32[512,3072]{1,0:T(8,128)}), f32[512,3072]{1,0:T(8,128)}) %all-reduce.6.cloned.1.call-update) | async-done | bytes 6291472 | tf_op jit(solution)/shard_map/psum | solution.py:87
  637.3 9.5 %multiply_reduce_fusion.1 = (f32[]{:T(128)}, f32[512,3072]{1,0:T(8,128)S(1)}) fusion(f32[512,3072]{1,0:T(8,128)} %all-reduce.6.cloned.1.call-done, f32[512,3072]{1,0:T(8,128)} %all-reduce.4.cloned.1.call-done, f32[512,3072]{1,0:T(8,128)} %all-gather.23.cloned.1.call-done), kind=kLoop, calls=%fused_computation.16 | loop fusion | flops 6291455 | bytes 25165828 | tf_op jit(solution)/shard_map/reduce_sum | solution.py:89
  646.8 2.6 copy-done.1
  649.4 10.6 %fusion = f32[384,3072]{1,0:T(8,128)} fusion(f32[512,3072]{1,0:T(8,128)S(1)} %get-tuple-element.745, f32[512,384]{1,0:T(8,128)} %copy-done.2), kind=kOutput, calls=%fused_computation.20 | convolution fusion | flops 7250116608 | bytes 11796480 | tf_op jit(solution)/shard_map/dot_general | solution.py:91
  660.1 0.3 reduce-scatter.3.cloned.1.call-start
  660.4 0.8 copy-done.3
  661.2 14.1 %multiply_reduce_fusion.3 = (f32[384]{0:T(512)S(1)}, f32[512,384]{1,0:T(8,128)S(1)}) fusion(f32[512]{0:T(512)S(1)} %get-tuple-element.757, f32[512,384]{1,0:T(8,128)S(1)} %copy-done.3, f32[384,3072]{1,0:T(8,128)} %param.21, f32[512,3072]{1,0:T(8,128)} %copy-done.1), kind=kOutput, calls=%fused_computation.44 | convolution fusion | flops 7251295744 | bytes 12586496 | tf_op jit(solution)/shard_map/dot_general | solution.py:98
  675.3 15.4 %fusion.26 = f32[3072,384]{1,0:T(8,128)} fusion(f32[512,384]{1,0:T(8,128)S(1)} %get-tuple-element.761, f32[512,3072]{1,0:T(8,128)} %all-reduce.4.cloned.1.call-done, f32[512,3072]{1,0:T(8,128)} %all-gather.23.cloned.1.call-done, f32[512]{0:T(512)S(1)} %get-tuple-element.757, f32[512]{0:T(512)S(1)} %get-tuple-element.756), kind=kOutput, calls=%fused_computation.76 | convolution fusion | flops 7252475904 | bytes 18092032 | tf_op jit(solution)/shard_map/dot_general | solution.py:106
  690.7 2.1 constant_dynamic-slice_fusion.6
  692.8 10.5 %all-reduce = (f32[384]{0:T(512)}, f32[]{:T(128)}) all-reduce(f32[384]{0:T(512)S(1)} %get-tuple-element.760, f32[]{:T(128)} %get-tuple-element.744), channel_id=1, replica_groups=mesh['row'=4,'col'=8] {'row'}, use_global_device_ids=true, to_apply=%region_26.0 | all-reduce | flops 385 | bytes 3080 | tf_op jit(solution)/shard_map/psum | solution.py:114
  703.9 13.4 %reduce-scatter.5.cloned.1.call-done = f32[384,768]{1,0:T(8,128)} async-done(((f32[384,3072]{1,0:T(8,128)}), f32[384,768]{1,0:T(8,128)}) %reduce-scatter.5.cloned.1.call-update) | async-done | bytes 1179664 | tf_op jit(solution)/shard_map/reduce_scatter | solution.py:112
  717.3 60.4 %reduce-scatter.3.cloned.1.call-done = f32[768,384]{1,0:T(8,128)} async-done(((f32[3072,384]{1,0:T(8,128)}), f32[768,384]{1,0:T(8,128)}) %reduce-scatter.3.cloned.1.call-update) | async-done | bytes 1179664 | tf_op jit(solution)/shard_map/reduce_scatter | solution.py:111
  (111 shorter events, 1.8 us)
Async XLA Ops:
  7.2 69.9 %all-gather.23.cloned.1.call-start = ((), (), s32[]{:S(2)}) async-start(), calls=%async_computation.2 | async-start | bytes 7077888 | tf_op jit(solution)/shard_map/all_gather | solution.py:45
  7.9 165.9 %all-gather.25.cloned.1.call-start = ((), (), s32[]{:S(2)}) async-start(), calls=%async_computation.3 | async-start | bytes 11796480 | tf_op jit(solution)/shard_map/all_gather | solution.py:46
  8.6 464.9 %all-reduce.4.cloned.1.call-start = ((), (), s32[]{:S(2)}) async-start(), calls=%async_computation.4 | async-start | bytes 12582912 | tf_op jit(solution)/shard_map/psum | solution.py:75
  173.8 5.5 copy-start
  266.7 73.1 %copy-start.5 = (f32[512]{0:T(512)}, f32[512]{0:T(512)S(1)}, u32[]{:S(2)}) copy-start(f32[512]{0:T(512)S(1)} %add_subtract_fusion.2) | copy-start | bytes 6148
  293.9 45.8 %copy-start.4 = (f32[768]{0:T(1024)}, f32[768]{0:T(1024)S(1)}, u32[]{:S(2)}) copy-start(f32[768]{0:T(1024)S(1)} %add_subtract_fusion) | copy-start | bytes 9220
  339.8 0.7 copy-start.6
  339.8 133.8 %copy-start.7 = (f32[384]{0:T(512)S(1)}, f32[384]{0:T(512)}, u32[]{:S(2)}) copy-start(f32[384]{0:T(512)} %param.20) | copy-start | bytes 4612
  339.8 149.3 %slice-start = ((s8[4718592]{0:T(1024)(128)(4,1)}), s8[524288]{0:T(1024)(128)(4,1)S(1)}, s32[]{:S(2)}) async-start(s8[4718592]{0:T(1024)(128)(4,1)} %bitcast.67), calls=%async_computation.8 | async-start | bytes 1048576
  339.8 297.5 %all-reduce.6.cloned.1.call-start = ((), (), s32[]{:S(2)}) async-start(), calls=%async_computation.5 | async-start | bytes 12582912 | tf_op jit(solution)/shard_map/psum | solution.py:87
  473.6 15.5 %slice-start.1 = ((s8[4718592]{0:T(1024)(128)(4,1)}), s8[4194304]{0:T(1024)(128)(4,1)S(1)}, s32[]{:S(2)}) async-start(s8[4718592]{0:T(1024)(128)(4,1)} %bitcast.67), calls=%async_computation.9 | async-start | bytes 8388608
  488.2 0.9 copy-start.2
  501.1 216.2 %reduce-scatter.5.cloned.1.call-start = ((), (), s32[]{:S(2)}) async-start(), calls=%async_computation.7 | async-start | bytes 5898240 | tf_op jit(solution)/shard_map/reduce_scatter | solution.py:112
  646.8 2.6 copy-start.1
  660.1 1.1 copy-start.3
  660.1 117.6 %reduce-scatter.3.cloned.1.call-start = ((), (), s32[]{:S(2)}) async-start(), calls=%async_computation.6 | async-start | bytes 5898240 | tf_op jit(solution)/shard_map/reduce_scatter | solution.py:111
Sparse Core Ops, SparseCore 0:
  9.6 67.4 all-gather.22
  78.9 94.8 all-gather.24
  339.9 133.6 all-reduce.3
  501.2 136.0 all-reduce.5
  660.2 57.0 reduce-scatter.4
  720.7 56.9 reduce-scatter.2
where the time goes:
time: 794 us; the launch traced here: 786 us
  waiting for transfers between devices  506 us (64%)
  blocking collectives  129 us (16%)
  matrix products  104 us (13%)
  other arithmetic  20.5 us (3%)
  between operations  16.6 us (2%)
  local copies, waits for them, and re-layouts  8.41 us (1%)
    psum x1, waiting for transfers between devices, body(): out = lax.psum(part_out, 'col')  136 us
    psum x1, waiting for transfers between devices, body(): whole_targets = lax.psum(partial_value, 'col')  133 us
    all_gather x10, blocking collectives, merged(): everything = jax.tree.map(lambda part: lax.all_gather(part, axis), array)  118 us
    all_gather x1, waiting for transfers between devices, body(): full_images = lax.all_gather(images, 'row', axis=1, tiled=True)  93.5 us
    all_gather x1, waiting for transfers between devices, body(): full_noise = lax.all_gather(noise, 'col', axis=1, tiled=True)  68.3 us
    reduce_scatter x1, waiting for transfers between devices, body(): lax.psum_scatter(local_in, 'row', scatter_dimension=0, tiled=True)  60.4 us
    dot_general x1, matrix products, body(): jnp.dot(weights, full_images, precision=highest, preferred_element_type=j...  19.3 us
    dot_general x1, matrix products, body(): lax.dot_general(full_noise, full_images, (((1,), (1,)), ((), ())), precis...  18.3 us
  transfers between devices with their start and end apart: 6, of which 6 were waited for; matrix products, arithmetic and copies ran while one was open for 4% of the time, Pallas kernels for 0%

commit v1 on v0

--- a/solution.py
+++ b/solution.py
@@ -42,7 +42,9 @@
 
 def body(noise, images, time_index, w_in, time_gain, w_out):
     highest = lax.Precision.HIGHEST
-    full_noise = lax.all_gather(noise, "col", axis=1, tiled=True)
+    full_noise = jnp.concatenate(
+        lax.all_to_all(jnp.stack([noise] * lax.axis_size("col")), "col", 0, 0), axis=1
+    )
     full_images = lax.all_gather(images, "row", axis=1, tiled=True)
     width = full_noise.shape[1]
     noise_count = full_noise.shape[0] * lax.axis_size("row")

time: 794 us -> 778 us (0.980)
  waiting for transfers between devices: 506 us -> 483 us
  blocking collectives: 129 us -> 120 us
    all_to_all x0 -> x1, waiting for transfers between devices: none -> 139 us  [body(): lax.all_to_all(jnp.stack([noise] * lax.axis_size('col')), 'col', 0, 0)]
    all_gather x1, waiting for transfers between devices: 93.5 us -> 0.02 us  [body(): full_images = lax.all_gather(images, 'row', axis=1, tiled=True)]
    all_gather x1 -> x0, waiting for transfers between devices: 68.3 us -> none  [body(): full_noise = lax.all_gather(noise, 'col', axis=1, tiled=True)]
    all_gather x10, blocking collectives: 118 us -> 109 us  [merged(): everything = jax.tree.map(lambda part: lax.all_gather(part, axis), array)]
  transfers between devices with their start and end apart: 6 -> 6, of which waited for: 6 -> 5; matrix products, arithmetic and copies ran while one was open for 4% -> 6% of each run, Pallas kernels for 0% -> 0%
where the time goes in v1:
time: 778 us; the launch traced here: 770 us
  waiting for transfers between devices  483 us (62%)
  blocking collectives  120 us (15%)
  matrix products  105 us (13%)
  other arithmetic  23.7 us (3%)
  between operations  16.3 us (2%)
  local copies, waits for them, and re-layouts  14.4 us (2%)
    all_to_all x1, waiting for transfers between devices, body(): lax.all_to_all(jnp.stack([noise] * lax.axis_size('col')), 'col', 0, 0)  139 us
    psum x1, waiting for transfers between devices, body(): out = lax.psum(part_out, 'col')  136 us
    psum x1, waiting for transfers between devices, body(): whole_targets = lax.psum(partial_value, 'col')  133 us
    all_gather x10, blocking collectives, merged(): everything = jax.tree.map(lambda part: lax.all_gather(part, axis), array)  109 us
    reduce_scatter x1, waiting for transfers between devices, body(): lax.psum_scatter(local_in, 'row', scatter_dimension=0, tiled=True)  60.4 us
    dot_general x1, matrix products, body(): jnp.dot(weights, full_images, precision=highest, preferred_element_type=j...  19.3 us
    dot_general x1, matrix products, body(): lax.dot_general(full_noise, full_images, (((1,), (1,)), ((), ())), precis...  18.3 us
  transfers between devices with their start and end apart: 6, of which 5 were waited for; matrix products, arithmetic and copies ran while one was open for 6% of the time, Pallas kernels for 0%

profile of v1, /device:TPU:0, one launch (start us, length us, event | category | flops | bytes accessed | tf_op | source)
XLA Modules:
  0.0 769.9 jit_solution(1087133708891520876)
XLA Ops:
  7.2 0.7 all-gather.22.cloned.1.call-update
  7.9 4.2 stack.2
  12.1 6.4 all-to-all-start
  18.5 139.0 %all-to-all-done = f32[8,512,384]{2,1,0:T(8,128)} async-done(((f32[8,512,384]{2,1,0:T(8,128)}), f32[8,512,384]{2,1,0:T(8,128)}, u32[]{:S(2)}, u32[]{:S(2)}) %all-to-all-start) | async-done | bytes 6291488 | tf_op jit(solution)/shard_map/all_to_all | solution.py:46
  157.5 6.3 copy.24
  163.8 3.3 fusion
  167.1 4.5 multiply_reduce_fusion
  171.6 0.9 copy-done
  172.5 18.3 %subtract_reduce_fusion.3 = (f32[512]{0:T(512)S(1)}, f32[512,768]{1,0:T(8,128)S(1)}) fusion(f32[512,3072]{1,0:T(8,128)S(1)} %bitcast.76, f32[768,3072]{1,0:T(8,128)} %all-gather.22.cloned.1.call-done, f32[768]{0:T(1024)S(1)} %multiply_reduce_fusion, f32[512]{0:T(512)S(1)} %fusion), kind=kOutput, calls=%fused_computation.39 | convolution fusion | flops 14497873920 | bytes 17308672 | tf_op jit(solution)/shard_map/dot_general | solution.py:54
  190.8 0.4 exponential_reduce_fusion.4
  191.2 12.8 %all-gather.11 = f32[8,1,512]{2,1,0:T(1,128)S(1)} all-gather(f32[1,1,512]{2,1,0:T(1,128)S(1)} %bitcast.105), channel_id=3, replica_groups=mesh['row'=4,'col'=8] {'col'}, dimensions={0}, use_global_device_ids=true | all-gather | bytes 18432 | tf_op jit(solution)/shard_map/all_gather | solution.py:12
  204.0 12.8 %all-gather.10 = f32[8,1,512]{2,1,0:T(1,128)S(1)} all-gather(f32[1,1,512]{2,1,0:T(1,128)S(1)} %bitcast.103), channel_id=2, replica_groups=mesh['row'=4,'col'=8] {'col'}, dimensions={0}, use_global_device_ids=true | all-gather | bytes 18432 | tf_op jit(solution)/shard_map/all_gather | solution.py:12
  216.8 0.4 while.85
  217.4 0.3 exponential_reduce_fusion.3
  217.7 8.2 %all-gather.13 = f32[4,1,768]{2,1,0:T(1,128)S(1)} all-gather(f32[1,1,768]{2,1,0:T(1,128)S(1)} %reshape.75), channel_id=5, replica_groups=mesh['row'=4,'col'=8] {'row'}, dimensions={0}, use_global_device_ids=true | all-gather | bytes 15360 | tf_op jit(solution)/shard_map/all_gather | solution.py:12
  225.9 8.2 %all-gather.12 = f32[4,1,768]{2,1,0:T(1,128)S(1)} all-gather(f32[1,1,768]{2,1,0:T(1,128)S(1)} %reshape.73), channel_id=4, replica_groups=mesh['row'=4,'col'=8] {'row'}, dimensions={0}, use_global_device_ids=true | all-gather | bytes 15360 | tf_op jit(solution)/shard_map/all_gather | solution.py:12
  234.1 0.2 while.86
  234.4 0.2 subtract_reduce_fusion.1
  234.5 0.4 exponential_reduce_fusion.2
  235.0 12.8 %all-gather.15 = f32[8,1,512]{2,1,0:T(1,128)S(1)} all-gather(f32[1,1,512]{2,1,0:T(1,128)S(1)} %bitcast.104), channel_id=7, replica_groups=mesh['row'=4,'col'=8] {'col'}, dimensions={0}, use_global_device_ids=true | all-gather | bytes 18432 | tf_op jit(solution)/shard_map/all_gather | solution.py:12
  247.7 13.2 %all-gather.14 = f32[8,1,512]{2,1,0:T(1,128)S(1)} all-gather(f32[1,1,512]{2,1,0:T(1,128)S(1)} %bitcast.101), channel_id=6, replica_groups=mesh['row'=4,'col'=8] {'col'}, dimensions={0}, use_global_device_ids=true | all-gather | bytes 18432 | tf_op jit(solution)/shard_map/all_gather | solution.py:12
  261.0 0.4 while.87
  261.6 0.3 exponential_reduce_fusion.1
  261.9 7.2 all-gather.17
  269.2 8.2 %all-gather.16 = f32[4,1,768]{2,1,0:T(1,128)S(1)} all-gather(f32[1,1,768]{2,1,0:T(1,128)S(1)} %reshape.81), channel_id=8, replica_groups=mesh['row'=4,'col'=8] {'row'}, dimensions={0}, use_global_device_ids=true | all-gather | bytes 15360 | tf_op jit(solution)/shard_map/all_gather | solution.py:12
  277.3 0.2 while.88
  277.6 0.2 subtract_reduce_fusion.4
  277.8 0.4 exponential_reduce_fusion
  278.2 12.8 %all-gather.19 = f32[8,1,512]{2,1,0:T(1,128)S(1)} all-gather(f32[1,1,512]{2,1,0:T(1,128)S(1)} %bitcast.106), channel_id=11, replica_groups=mesh['row'=4,'col'=8] {'col'}, dimensions={0}, use_global_device_ids=true | all-gather | bytes 18432 | tf_op jit(solution)/shard_map/all_gather | solution.py:12
  291.0 12.8 %all-gather.18 = f32[8,1,512]{2,1,0:T(1,128)S(1)} all-gather(f32[1,1,512]{2,1,0:T(1,128)S(1)} %bitcast.102), channel_id=10, replica_groups=mesh['row'=4,'col'=8] {'col'}, dimensions={0}, use_global_device_ids=true | all-gather | bytes 18432 | tf_op jit(solution)/shard_map/all_gather | solution.py:12
  303.7 0.4 while.89
  304.1 19.3 %fusion.7 = f32[512,3072]{1,0:T(8,128)} fusion(f32[768,3072]{1,0:T(8,128)} %all-gather.22.cloned.1.call-done, f32[512,768]{1,0:T(8,128)S(1)} %get-tuple-element.759, f32[512]{0:T(512)S(1)} %log_add_fusion, f32[768]{0:T(1024)S(1)} %add_subtract_fusion), kind=kOutput, calls=%fused_computation.27 | convolution fusion | flops 14496301056 | bytes 17306624 | tf_op jit(solution)/shard_map/dot_general | solution.py:72
  323.4 0.2 all-reduce.6.cloned.1.call-start
  323.7 0.4 copy-done.3
  324.1 133.1 %all-reduce.4.cloned.1.call-done = f32[512,3072]{1,0:T(8,128)} async-done(((f32[512,3072]{1,0:T(8,128)}), f32[512,3072]{1,0:T(8,128)}) %all-reduce.4.cloned.1.call-update) | async-done | bytes 6291472 | tf_op jit(solution)/shard_map/psum | solution.py:77
  457.2 14.5 %convolution_add_fusion = f32[512,384]{1,0:T(8,128)S(1)} fusion(f32[3072,384]{1,0:T(8,128)} %param.19, f32[384]{0:T(512)S(1)} %copy-done.4, f32[512]{0:T(512)S(1)} %get-tuple-element.757, f32[512,3072]{1,0:T(8,128)} %all-reduce.4.cloned.1.call-done, f32[512,3072]{1,0:T(8,128)} %bitcast.73, f32[512]{0:T(512)S(1)} %get-tuple-element.756), kind=kOutput, calls=%fused_computation.44 | convolution fusion | flops 7252869120 | bytes 18093568 | tf_op jit(solution)/shard_map/dot_general | solution.py:83
  471.8 12.0 %fusion.21 = f32[512,3072]{1,0:T(8,128)} fusion(f32[384,3072]{1,0:T(8,128)S(1)} %bitcast.78, f32[512,384]{1,0:T(8,128)S(1)} %convolution_add_fusion), kind=kOutput, calls=%fused_computation.50 | convolution fusion | flops 7248543744 | bytes 11796480 | tf_op jit(solution)/shard_map/dot_general | solution.py:88
  483.8 0.3 reduce-scatter.5.cloned.1.call-start
  484.1 136.0 %all-reduce.6.cloned.1.call-done = f32[512,3072]{1,0:T(8,128)} async-done(((f32[512,3072]{1,0:T(8,128)}), f32[512,3072]{1,0:T(8,128)}) %all-reduce.6.cloned.1.call-update) | async-done | bytes 6291472 | tf_op jit(solution)/shard_map/psum | solution.py:89
  620.1 12.7 %multiply_reduce_fusion.1 = (f32[]{:T(128)}, f32[512,3072]{1,0:T(8,128)}) fusion(f32[512,3072]{1,0:T(8,128)} %all-reduce.6.cloned.1.call-done, f32[512,3072]{1,0:T(8,128)} %all-reduce.4.cloned.1.call-done, f32[512,3072]{1,0:T(8,128)} %bitcast.74), kind=kLoop, calls=%fused_computation.18 | loop fusion | flops 6291455 | bytes 25165828 | tf_op jit(solution)/shard_map/reduce_sum | solution.py:91
  632.8 11.3 %fusion.1 = f32[384,3072]{1,0:T(8,128)} fusion(f32[512,3072]{1,0:T(8,128)} %get-tuple-element.745, f32[512,384]{1,0:T(8,128)S(1)} %convolution_add_fusion), kind=kOutput, calls=%fused_computation.21 | convolution fusion | flops 7250116608 | bytes 11796480 | tf_op jit(solution)/shard_map/dot_general | solution.py:93
  644.1 0.3 reduce-scatter.3.cloned.1.call-start
  644.4 14.1 %multiply_reduce_fusion.2 = (f32[384]{0:T(512)S(1)}, f32[512,384]{1,0:T(8,128)S(1)}) fusion(f32[512]{0:T(512)S(1)} %get-tuple-element.757, f32[512,384]{1,0:T(8,128)S(1)} %convolution_add_fusion, f32[384,3072]{1,0:T(8,128)} %param.21, f32[512,3072]{1,0:T(8,128)} %get-tuple-element.745), kind=kOutput, calls=%fused_computation.45 | convolution fusion | flops 7251295744 | bytes 12586496 | tf_op jit(solution)/shard_map/dot_general | solution.py:100
  658.5 15.2 %fusion.27 = f32[3072,384]{1,0:T(8,128)} fusion(f32[512,384]{1,0:T(8,128)S(1)} %get-tuple-element.761, f32[512,3072]{1,0:T(8,128)} %all-reduce.4.cloned.1.call-done, f32[512,3072]{1,0:T(8,128)} %bitcast.75, f32[512]{0:T(512)S(1)} %get-tuple-element.757, f32[512]{0:T(512)S(1)} %get-tuple-element.756), kind=kOutput, calls=%fused_computation.77 | convolution fusion | flops 7252475904 | bytes 18092032 | tf_op jit(solution)/shard_map/dot_general | solution.py:108
  673.7 2.1 constant_dynamic-slice_fusion.6
  675.8 10.8 %all-reduce = (f32[384]{0:T(512)}, f32[]{:T(128)}) all-reduce(f32[384]{0:T(512)S(1)} %get-tuple-element.760, f32[]{:T(128)} %get-tuple-element.744), channel_id=1, replica_groups=mesh['row'=4,'col'=8] {'row'}, use_global_device_ids=true, to_apply=%region_26.0 | all-reduce | flops 385 | bytes 3080 | tf_op jit(solution)/shard_map/psum | solution.py:116
  687.2 14.2 %reduce-scatter.5.cloned.1.call-done = f32[384,768]{1,0:T(8,128)} async-done(((f32[384,3072]{1,0:T(8,128)}), f32[384,768]{1,0:T(8,128)}) %reduce-scatter.5.cloned.1.call-update) | async-done | bytes 1179664 | tf_op jit(solution)/shard_map/reduce_scatter | solution.py:114
  701.3 60.4 %reduce-scatter.3.cloned.1.call-done = f32[768,384]{1,0:T(8,128)} async-done(((f32[3072,384]{1,0:T(8,128)}), f32[768,384]{1,0:T(8,128)}) %reduce-scatter.3.cloned.1.call-update) | async-done | bytes 1179664 | tf_op jit(solution)/shard_map/reduce_scatter | solution.py:113
  (106 shorter events, 1.6 us)
Async XLA Ops:
  7.2 159.9 %all-gather.22.cloned.1.call-start = ((), (), s32[]{:S(2)}) async-start(), calls=%async_computation.3 | async-start | bytes 11796480 | tf_op jit(solution)/shard_map/all_gather | solution.py:48
  12.1 145.4 %all-to-all-start = ((f32[8,512,384]{2,1,0:T(8,128)}), f32[8,512,384]{2,1,0:T(8,128)}, u32[]{:S(2)}, u32[]{:S(2)}) async-start(f32[8,512,384]{2,1,0:T(8,128)} %stack.2), calls=%async_computation | async-start | bytes 12582912 | tf_op jit(solution)/shard_map/all_to_all | solution.py:46
  18.5 438.8 %all-reduce.4.cloned.1.call-start = ((), (), s32[]{:S(2)}) async-start(), calls=%async_computation.4 | async-start | bytes 12582912 | tf_op jit(solution)/shard_map/psum | solution.py:77
  167.1 5.5 copy-start
  261.4 62.0 %copy-start.2 = (f32[512]{0:T(512)}, f32[512]{0:T(512)S(1)}, u32[]{:S(2)}) copy-start(f32[512]{0:T(512)S(1)} %add_subtract_fusion.2) | copy-start | bytes 6148
  277.6 45.8 %copy-start.1 = (f32[768]{0:T(1024)}, f32[768]{0:T(1024)S(1)}, u32[]{:S(2)}) copy-start(f32[768]{0:T(1024)S(1)} %add_subtract_fusion) | copy-start | bytes 9220
  323.4 0.7 copy-start.3
  323.4 133.8 %copy-start.4 = (f32[384]{0:T(512)S(1)}, f32[384]{0:T(512)}, u32[]{:S(2)}) copy-start(f32[384]{0:T(512)} %param.20) | copy-start | bytes 4612
  323.4 148.4 %slice-start = ((s8[4718592]{0:T(1024)(128)(4,1)}), s8[524288]{0:T(1024)(128)(4,1)S(1)}, s32[]{:S(2)}) async-start(s8[4718592]{0:T(1024)(128)(4,1)} %bitcast.77), calls=%async_computation.8 | async-start | bytes 1048576
  323.4 296.6 %all-reduce.6.cloned.1.call-start = ((), (), s32[]{:S(2)}) async-start(), calls=%async_computation.5 | async-start | bytes 12582912 | tf_op jit(solution)/shard_map/psum | solution.py:89
  457.2 14.5 %slice-start.1 = ((s8[4718592]{0:T(1024)(128)(4,1)}), s8[4194304]{0:T(1024)(128)(4,1)S(1)}, s32[]{:S(2)}) async-start(s8[4718592]{0:T(1024)(128)(4,1)} %bitcast.77), calls=%async_computation.9 | async-start | bytes 8388608
  483.8 217.5 %reduce-scatter.5.cloned.1.call-start = ((), (), s32[]{:S(2)}) async-start(), calls=%async_computation.7 | async-start | bytes 5898240 | tf_op jit(solution)/shard_map/reduce_scatter | solution.py:114
  644.1 117.6 %reduce-scatter.3.cloned.1.call-start = ((), (), s32[]{:S(2)}) async-start(), calls=%async_computation.6 | async-start | bytes 5898240 | tf_op jit(solution)/shard_map/reduce_scatter | solution.py:113
Sparse Core Ops, SparseCore 0:
  9.8 98.9 all-gather.21
  323.6 133.6 all-reduce.3
  484.0 136.0 all-reduce.5
  644.3 57.0 reduce-scatter.4
  704.7 56.9 reduce-scatter.2
